TPU v7x, 256 devices: a whole 4x4x8 slice. The times are simulated.
256 devices in a mesh: video: 4 (over x), tm: 16 (over z, core), space: 4 (over y).
Axes of the slice: x: 4, y: 4, z: 8, core: 2. Of those that a mesh axis runs over, the one named last changes fastest.
Arguments:
- feature_maps: bfloat16 [64, 128, 240, 128], P(('video', 'tm'), 'space'), parts along dimension 0, may hold values from -27 to 27
- query_frame: int32 [2048], P('video'), parts along dimension 0, may hold values from 0 to 15
- query_row: int32 [2048], P('video'), parts along dimension 0, may hold values from 0 to 127
- query_col: int32 [2048], P('video'), parts along dimension 0, may hold values from 0 to 239
- ema_decay: float32 [64, 128], P(('video', 'tm')), parts along dimension 0, may hold values from 0.14 to 1
- dw_kernel: float32 [3, 128], replicated, may hold values from -3 to 3
- pw_weight: bfloat16 [128, 128], replicated, may hold values from -0.5 to 0.5
- out_weight: float32 [2, 128], replicated, may hold values from -2 to 2
Outputs:
- tracks: float32 [64, 2, 512], P(('video', 'tm')), parts along dimension 0
There are 4 independent parts, one for each index of `video`. A program takes and returns all parts, laid end to end along the dimension named above; an argument that names none is the same for every part. Nothing has to cross between parts.
All inputs are finite; a program needn't handle non-finite values.
Results may differ from a plain program's by a relative error of at most 0.0026.
Values may be sent and summed in bfloat16 or wider, within the bound.
A program may use at most 128 MiB of HBM per device.

v0:
```python
import math
import jax
import jax.numpy as jnp
from jax import lax
from jax.sharding import PartitionSpec as P


def with_halo(cells, sides, width):
    for axis, dim in sides:
        count = lax.axis_size(axis)
        ends = count - 1
        head = lax.slice_in_dim(cells, 0, width, axis=dim)
        tail = lax.slice_in_dim(cells, cells.shape[dim] - width, cells.shape[dim], axis=dim)
        cells = jnp.concatenate(
            [
                lax.ppermute(tail, axis, [(i, (i + 1) % count) for i in range(ends)]),
                cells,
                lax.ppermute(head, axis, [((i + 1) % count, i) for i in range(ends)]),
            ],
            axis=dim,
        )
    return cells


def local(
    feature_maps, query_frame, query_row, query_col, ema_decay, dw_kernel, pw_weight, out_weight
):
    frames_here, rows_here, map_width, channels = feature_maps.shape
    num_queries = query_frame.shape[0]
    first_frame = lax.axis_index("tm") * frames_here
    first_row = lax.axis_index("space") * rows_here
    map_height = rows_here * lax.axis_size("space")
    local_frame = query_frame - first_frame
    local_row = query_row - first_row
    owned = (
        (local_frame >= 0)
        & (local_frame < frames_here)
        & (local_row >= 0)
        & (local_row < rows_here)
    )
    picked = feature_maps[
        jnp.clip(local_frame, 0, frames_here - 1), jnp.clip(local_row, 0, rows_here - 1), query_col
    ]
    contrib = jnp.where(owned[:, None], picked.astype(jnp.float32), 0.0)
    query_feats = lax.psum(contrib, ("tm", "space")).astype(jnp.bfloat16)
    scale = 1.0 / math.sqrt(channels)
    col_coord = jnp.arange(map_width, dtype=jnp.int32).astype(jnp.float32) / map_width
    row_coord = (first_row + jnp.arange(rows_here, dtype=jnp.int32)).astype(
        jnp.float32
    ) / map_height
    highest_list, total_list, pos_list, feat_list = ([], [], [], [])
    frame_index = 0
    frame_map = feature_maps[frame_index].reshape(rows_here * map_width, channels)
    scores = (
        lax.dot_general(
            query_feats, frame_map, (((1,), (1,)), ((), ())), preferred_element_type=jnp.float32
        )
        * scale
    )
    highest = jnp.max(scores, axis=1)
    weights_exp = jnp.exp(scores - highest[:, None])
    highest_list.append(highest)
    total_list.append(jnp.sum(weights_exp, axis=1))
    grid = weights_exp.reshape(num_queries, rows_here, map_width)
    col_part = jnp.sum(jnp.sum(grid, axis=1) * col_coord[None, :], axis=1)
    line_portion = jnp.sum(jnp.sum(grid, axis=2) * row_coord[None, :], axis=1)
    pos_list.append(jnp.stack([col_part, line_portion], 1))
    feat_list.append(
        jnp.dot(weights_exp.astype(jnp.bfloat16), frame_map, preferred_element_type=jnp.float32)
    )
    highest = jnp.stack(highest_list)
    totals = jnp.stack(total_list)
    pos_sum = jnp.stack(pos_list)
    feat_sum = jnp.stack(feat_list)
    top_value = lax.pmax(highest, "space")
    factor = jnp.exp(highest - top_value)
    grand_total, pos_all, feat_all = lax.psum(
        (factor * totals, factor[..., None] * pos_sum, factor[..., None] * feat_sum), "space"
    )
    position = pos_all / grand_total[..., None]
    focused_result = (feat_all / grand_total[..., None]).astype(jnp.bfloat16)
    padded = with_halo(focused_result, (("tm", 0),), 1).astype(jnp.float32)
    depth = jnp.zeros((frames_here, num_queries, channels), jnp.float32)
    for tap in range(dw_kernel.shape[0]):
        depth = depth + dw_kernel[tap][None, None, :] * padded[tap : tap + frames_here]
    hidden = jax.nn.gelu(depth).astype(jnp.bfloat16)
    mixed = jnp.dot(
        hidden.reshape(-1, channels), pw_weight, preferred_element_type=jnp.float32
    ).reshape(frames_here, num_queries, channels)
    refined = focused_result.astype(jnp.float32) + mixed
    carried = jnp.zeros((num_queries, channels), jnp.float32)
    retain_prod = jnp.ones((channels,), jnp.float32)
    local_states, local_prods = ([], [])
    frame_index = 0
    retain = ema_decay[frame_index]
    carried = retain[None, :] * carried + (1.0 - retain[None, :]) * refined[frame_index]
    retain_prod = retain_prod * retain
    local_states.append(carried)
    local_prods.append(retain_prod)
    all_prods, all_ends = (
        lax.all_gather(retain_prod[None], "tm", axis=0, tiled=True),
        lax.all_gather(carried[None], "tm", axis=0, tiled=True),
    )
    position_tm = lax.axis_index("tm")

    def fold_step(source, running):
        advanced = all_prods[source][None, :] * running + all_ends[source]
        return jnp.where(source < position_tm, advanced, running)

    incoming = lax.fori_loop(
        0, lax.axis_size("tm"), fold_step, jnp.zeros((num_queries, channels), jnp.float32)
    )
    memory = jnp.stack(local_states) + jnp.stack(local_prods)[:, None, :] * incoming[None]
    delta = jnp.einsum("tqc,kc->tkq", memory, out_weight, precision=lax.Precision.HIGHEST)
    return jnp.transpose(position, (0, 2, 1)) + delta


def solution(mesh):
    placed = (
        P(("video", "tm"), "space", None, None),
        P("video"),
        P("video"),
        P("video"),
        P(("video", "tm"), None),
        P(),
        P(),
        P(),
    )
    return jax.shard_map(
        local, mesh=mesh, in_specs=placed, out_specs=P(("video", "tm"), None, None), check_vma=False
    )
```

profile of v0, /device:TPU:1, one launch (start us, length us, event | category | flops | bytes accessed | tf_op | source)
XLA Modules:
  0.0 416.0 jit_solution(9454271297745757524)
XLA Ops:
  8.1 3.1 gather_fusion
  11.4 250.4 %all-reduce.5 = bf16[512,128]{1,0:T(8,128)(2,1)S(1)} all-reduce(f32[512,128]{1,0:T(8,128)S(1)} %convert_select_fusion), channel_id=1, replica_groups=mesh['video'=4,'tm'=16,'space'=4] {'tm','space'}, use_global_device_ids=true, to_apply=%region_0.1 | all-reduce | flops 65536 | bytes 393216 | tf_op jit(solution)/shard_map/psum | solution.py:45
  261.8 2.3 multiply_reduce_fusion
  264.1 7.0 %fusion.50 = (f32[512]{0:T(512)S(1)}, f32[512,7680]{1,0:T(8,128)}) fusion(f32[512]{0:T(512)S(1)} %get-tuple-element.139, f32[512,7680]{1,0:T(8,128)S(1)} %get-tuple-element.140), kind=kLoop, calls=%fused_computation.74 | loop fusion | flops 11795968 | bytes 31461376 | tf_op jit(solution)/shard_map/reduce_sum | solution.py:63
  271.1 6.0 %pmax.7 = f32[1,512]{1,0:T(1,128)S(1)} all-reduce(f32[1,512]{1,0:T(1,128)S(1)} %bitcast.66), channel_id=1, replica_groups=mesh['video'=4,'tm'=16,'space'=4] {'space'}, use_global_device_ids=true, to_apply=%region_2.3 | all-reduce | flops 512 | bytes 4096 | tf_op jit(solution)/shard_map/pmax | solution.py:75
  277.1 8.4 %fusion.7 = f32[1,512,128]{2,1,0:T(8,128)} fusion(bf16[7680,128]{1,0:T(8,128)(2,1)S(1)} %bitcast.62, f32[512,7680]{1,0:T(8,128)} %get-tuple-element.135, f32[512]{0:T(512)S(1)} %bitcast.64), kind=kOutput, calls=%fused_computation.11 | convolution fusion | flops 1010630656 | bytes 17958912 | tf_op jit(solution)/shard_map/dot_general | solution.py:69
  285.5 15.7 %copy.10 = f32[512,7680]{0,1:T(8,128)} copy(f32[512,7680]{1,0:T(8,128)} %get-tuple-element.135) | data formatting | bytes 31457280 | tf_op jit(solution)/shard_map/exp | solution.py:61
  301.3 7.9 %fusion.48 = (f32[512,240]{0,1:T(8,128)S(1)}, f32[512,32]{0,1:T(8,128)S(1)}) fusion(f32[512,32,240]{0,2,1:T(8,128)} %bitcast.63), kind=kLoop, calls=%fused_computation.72 | loop fusion | flops 7725056 | bytes 16285696 | tf_op jit(solution)/shard_map/reduce_sum | solution.py:65
  309.4 7.5 %all-reduce = (f32[512]{0:T(512)S(1)}, f32[1,512,2]{1,2,0:T(2,128)S(1)}) all-reduce(f32[512]{0:T(512)S(1)} %bitcast.70, f32[1,512,2]{1,2,0:T(2,128)S(1)} %maximum_multiply_fusion), channel_id=1, replica_groups=mesh['video'=4,'tm'=16,'space'=4] {'space'}, use_global_device_ids=true, to_apply=%region_9.10 | all-reduce | flops 1536 | bytes 12288 | tf_op jit(solution)/shard_map/psum | solution.py:77
  317.0 15.6 %all-reduce.4.cloned.1.call-done = f32[1,512,128]{2,1,0:T(8,128)} async-done(((f32[1,512,128]{2,1,0:T(8,128)}), f32[1,512,128]{2,1,0:T(8,128)}) %all-reduce.4.cloned.1.call-update) | async-done | bytes 262160 | tf_op jit(solution)/shard_map/psum | solution.py:77
  333.7 4.7 %collective-permute-start.1 = (bf16[1,512,128]{2,1,0:T(8,128)(2,1)S(1)}, bf16[1,512,128]{2,1,0:T(8,128)(2,1)S(1)}, u32[]{:S(2)}, u32[]{:S(2)}) collective-permute-start(bf16[1,512,128]{2,1,0:T(8,128)(2,1)S(1)} %divide_convert_fusion), channel_id=1, source_target_pairs={{4,0},{8,4},{12,8},{16,12},{20,16},{24,20},{28,24},{32,28},{36,32}... | collective-permute-start | bytes 393224 | tf_op jit(solution)/shard_map/ppermute | solution.py:18
  338.4 3.1 collective-permute-start
  342.2 1.2 collective-permute-done
  344.5 18.6 %all-gather = f32[16,1,128]{2,1,0:T(1,128)S(1)} all-gather(f32[1,1,128]{2,1,0:T(1,128)S(1)} %bitcast.73), channel_id=1, replica_groups=mesh['video'=4,'tm'=16,'space'=4] {'tm'}, dimensions={0}, use_global_device_ids=true | all-gather | bytes 8704 | tf_op jit(solution)/shard_map/all_gather | solution.py:101
  363.0 26.2 %all-gather.3.cloned.1.call-done = f32[16,512,128]{2,1,0:T(8,128)} async-done(((f32[1,512,128]{2,1,0:T(8,128)}), f32[16,512,128]{2,1,0:T(8,128)}) %all-gather.3.cloned.1.call-update) | async-done | bytes 4194320 | tf_op jit(solution)/shard_map/all_gather | solution.py:102
  389.2 19.0 %while.14 = (s32[]{:T(128)}, f32[512,128]{1,0:T(8,128)S(1)}, s32[]{:T(128)}, f32[16,128]{1,0:T(8,128)S(1)}, f32[16,512,128]{2,1,0:T(8,128)}, /*index=5*/s32[]{:T(128)}, s32[]{:T(128)}) while((s32[]{:T(128)}, f32[512,128]{1,0:T(8,128)S(1)}, s32[]{:T(128)}, f32[16,128]{1,0:T(8,128)S(1)}, f32[16,512,128]{2,1,0:T(8,128)}, ...), condition=%wide.region_12.13_spmd.clone, body=%wide.region_11.12_spmd.clone.sunk | while | flops 262148 | bytes 788081 | solution.py:110
  390.4 1.1 fusion.57
  391.6 1.1 fusion.57
  392.8 1.1 fusion.57
  394.0 1.1 fusion.57
  396.3 1.1 fusion.57
  397.5 1.1 fusion.57
  401.1 1.1 fusion.57
  404.7 1.1 fusion.57
  (56 shorter events, 15.1 us)
Async XLA Ops:
  6.5 1.6 copy-start
  6.5 326.1 %all-reduce.4.cloned.1.call-start = ((), (), s32[]{:S(2)}) async-start(), calls=%async_computation | async-start | bytes 524288 | tf_op jit(solution)/shard_map/psum | solution.py:77
  285.5 103.7 %all-gather.3.cloned.1.call-start = ((), (), s32[]{:S(2)}) async-start(), calls=%async_computation.1 | async-start | bytes 4456448 | tf_op jit(solution)/shard_map/all_gather | solution.py:102
  301.3 8.1 %copy-start.1 = (f32[1,128]{1,0:T(1,128)S(1)}, f32[1,128]{1,0:T(1,128)}, u32[]{:S(2)}) copy-start(f32[1,128]{1,0:T(1,128)} %param.14) | copy-start | bytes 1540
  301.3 15.7 %copy-start.2 = (f32[3,128]{1,0:T(4,128)S(1)}, f32[3,128]{1,0:T(4,128)}, u32[]{:S(2)}) copy-start(f32[3,128]{1,0:T(4,128)} %param.15) | copy-start | bytes 4612
  301.3 42.2 %copy-start.4 = (bf16[128,128]{1,0:T(8,128)(2,1)S(1)}, bf16[128,128]{1,0:T(8,128)(2,1)}, u32[]{:S(2)}) copy-start(bf16[128,128]{1,0:T(8,128)(2,1)} %param.16) | copy-start | bytes 98308
  301.3 106.9 %copy-start.3 = (f32[2,128]{1,0:T(2,128)S(1)}, f32[2,128]{1,0:T(2,128)}, u32[]{:S(2)}) copy-start(f32[2,128]{1,0:T(2,128)} %param.17) | copy-start | bytes 3076
  333.7 8.5 %collective-permute-start.1 = (bf16[1,512,128]{2,1,0:T(8,128)(2,1)S(1)}, bf16[1,512,128]{2,1,0:T(8,128)(2,1)S(1)}, u32[]{:S(2)}, u32[]{:S(2)}) collective-permute-start(bf16[1,512,128]{2,1,0:T(8,128)(2,1)S(1)} %divide_convert_fusion), channel_id=1, source_target_pairs={{4,0},{8,4},{12,8},{16,12},{20,16},{24,20},{28,24},{32,28},{36,32}... | collective-permute-start | bytes 393224 | tf_op jit(solution)/shard_map/ppermute | solution.py:18
  338.4 5.0 %collective-permute-start = (bf16[1,512,128]{2,1,0:T(8,128)(2,1)S(1)}, bf16[1,512,128]{2,1,0:T(8,128)(2,1)S(1)}, u32[]{:S(2)}, u32[]{:S(2)}) collective-permute-start(bf16[1,512,128]{2,1,0:T(8,128)(2,1)S(1)} %divide_convert_fusion), channel_id=1, source_target_pairs={{0,4},{4,8},{8,12},{12,16},{16,20},{20,24},{24,28},{28,32},{32,36}... | collective-permute-start | bytes 393224 | tf_op jit(solution)/shard_map/ppermute | solution.py:16
Sparse Core Ops, SparseCore 0:
  285.6 46.9 all-reduce.3
  344.6 44.5 all-gather.2
where the time goes:
time: 417 us; the launch traced here: 416 us
  blocking collectives  282 us (68%)
  waiting for transfers between devices  43.7 us (10%)
  other arithmetic  36.3 us (9%)
  local copies, waits for them, and re-layouts  19 us (5%)
  between operations  13.6 us (3%)
  matrix products  12.6 us (3%)
  starting transfers between devices  7.84 us (2%)
    psum x1, blocking collectives, local(): query_feats = lax.psum(contrib, ('tm', 'space')).astype(jnp.bfloat16)  250 us
    all_gather x1, waiting for transfers between devices, local(): lax.all_gather(carried[None], 'tm', axis=0, tiled=True)  26.2 us
    all_gather x1, blocking collectives, local(): lax.all_gather(retain_prod[None], 'tm', axis=0, tiled=True)  18.6 us
    select_n x16, other arithmetic, fold_step(): return jnp.where(source < position_tm, advanced, running)  18.4 us
    exp x1, local copies, waits for them, and re-layouts, local(): weights_exp = jnp.exp(scores - highest[:, None])  15.7 us
    psum x1, waiting for transfers between devices, local(): lax.psum((factor * totals, factor[..., None] * pos_sum, factor[..., None]...  15.6 us
    dot_general x1, matrix products, local(): jnp.dot(weights_exp.astype(jnp.bfloat16), frame_map, preferred_element_ty...  8.38 us
  transfers between devices with their start and end apart: 4, of which 4 were waited for; matrix products, arithmetic and copies ran while one was open for 6% of the time, Pallas kernels for 0%

commit v1 on v0

--- a/solution.py
+++ b/solution.py
@@ -99,7 +99,9 @@
     local_prods.append(retain_prod)
     all_prods, all_ends = (
         lax.all_gather(retain_prod[None], "tm", axis=0, tiled=True),
-        lax.all_gather(carried[None], "tm", axis=0, tiled=True),
+        jnp.concatenate(
+            lax.all_to_all(jnp.stack([carried[None]] * lax.axis_size("tm")), "tm", 0, 0), axis=0
+        ),
     )
     position_tm = lax.axis_index("tm")
 

time: 417 us -> 488 us (1.17)
  blocking collectives: 282 us -> 368 us
  waiting for transfers between devices: 43.7 us -> 17.6 us
  starting transfers between devices: 7.84 us -> 17.3 us
    all_gather x1, blocking collectives: 18.6 us -> 104 us  [local(): lax.all_gather(retain_prod[None], 'tm', axis=0, tiled=True)]
    all_gather x1 -> x0, waiting for transfers between devices: 26.2 us -> none  [local(): lax.all_gather(carried[None], 'tm', axis=0, tiled=True)]
    all_to_all x0 -> x1, starting transfers between devices: none -> 9.52 us  [local(): lax.all_to_all(jnp.stack([carried[None]] * lax.axis_size('tm')), 'tm', 0, 0)]
  transfers between devices with their start and end apart: 4 -> 4, of which waited for: 4 -> 3; matrix products, arithmetic and copies ran while one was open for 6% -> 5% of each run, Pallas kernels for 0% -> 0%
where the time goes in v1:
time: 488 us; the launch traced here: 487 us
  blocking collectives  368 us (75%)
  other arithmetic  36.4 us (7%)
  local copies, waits for them, and re-layouts  21.4 us (4%)
  waiting for transfers between devices  17.6 us (4%)
  starting transfers between devices  17.3 us (4%)
  between operations  13.6 us (3%)
  matrix products  11.9 us (2%)
    psum x1, blocking collectives, local(): query_feats = lax.psum(contrib, ('tm', 'space')).astype(jnp.bfloat16)  250 us
    all_gather x1, blocking collectives, local(): lax.all_gather(retain_prod[None], 'tm', axis=0, tiled=True)  104 us
    select_n x16, other arithmetic, fold_step(): return jnp.where(source < position_tm, advanced, running)  18.4 us
    exp x1, local copies, waits for them, and re-layouts, local(): weights_exp = jnp.exp(scores - highest[:, None])  15.7 us
    psum x1, waiting for transfers between devices, local(): lax.psum((factor * totals, factor[..., None] * pos_sum, factor[..., None]...  15.6 us
  transfers between devices with their start and end apart: 4, of which 3 were waited for; matrix products, arithmetic and copies ran while one was open for 5% of the time, Pallas kernels for 0%

profile of v1, /device:TPU:1, one launch (start us, length us, event | category | flops | bytes accessed | tf_op | source)
XLA Modules:
  0.0 487.0 jit_solution(1266831229400419627)
XLA Ops:
  8.1 3.1 gather_fusion
  11.4 250.4 %all-reduce.5 = bf16[512,128]{1,0:T(8,128)(2,1)S(1)} all-reduce(f32[512,128]{1,0:T(8,128)S(1)} %convert_select_fusion), channel_id=1, replica_groups=mesh['video'=4,'tm'=16,'space'=4] {'tm','space'}, use_global_device_ids=true, to_apply=%region_0.1 | all-reduce | flops 65536 | bytes 393216 | tf_op jit(solution)/shard_map/psum | solution.py:45
  261.8 2.3 multiply_reduce_fusion
  264.1 7.0 %fusion.50 = (f32[512]{0:T(512)S(1)}, f32[512,7680]{1,0:T(8,128)}) fusion(f32[512]{0:T(512)S(1)} %get-tuple-element.139, f32[512,7680]{1,0:T(8,128)S(1)} %get-tuple-element.140), kind=kLoop, calls=%fused_computation.74 | loop fusion | flops 11795968 | bytes 31461376 | tf_op jit(solution)/shard_map/reduce_sum | solution.py:63
  271.1 6.0 %pmax.7 = f32[1,512]{1,0:T(1,128)S(1)} all-reduce(f32[1,512]{1,0:T(1,128)S(1)} %bitcast.67), channel_id=1, replica_groups=mesh['video'=4,'tm'=16,'space'=4] {'space'}, use_global_device_ids=true, to_apply=%region_2.3 | all-reduce | flops 512 | bytes 4096 | tf_op jit(solution)/shard_map/pmax | solution.py:75
  277.1 8.4 %fusion.7 = f32[1,512,128]{2,1,0:T(8,128)} fusion(bf16[7680,128]{1,0:T(8,128)(2,1)S(1)} %bitcast.63, f32[512,7680]{1,0:T(8,128)} %get-tuple-element.135, f32[512]{0:T(512)S(1)} %bitcast.65), kind=kOutput, calls=%fused_computation.11 | convolution fusion | flops 1010630656 | bytes 17958912 | tf_op jit(solution)/shard_map/dot_general | solution.py:69
  285.5 15.7 %copy.10 = f32[512,7680]{0,1:T(8,128)} copy(f32[512,7680]{1,0:T(8,128)} %get-tuple-element.135) | data formatting | bytes 31457280 | tf_op jit(solution)/shard_map/exp | solution.py:61
  301.2 7.9 %fusion.48 = (f32[512,240]{0,1:T(8,128)S(1)}, f32[512,32]{0,1:T(8,128)S(1)}) fusion(f32[512,32,240]{0,2,1:T(8,128)} %bitcast.64), kind=kLoop, calls=%fused_computation.72 | loop fusion | flops 7725056 | bytes 16285696 | tf_op jit(solution)/shard_map/reduce_sum | solution.py:65
  309.4 7.5 %all-reduce = (f32[512]{0:T(512)S(1)}, f32[1,512,2]{1,2,0:T(2,128)S(1)}) all-reduce(f32[512]{0:T(512)S(1)} %bitcast.71, f32[1,512,2]{1,2,0:T(2,128)S(1)} %maximum_multiply_fusion), channel_id=1, replica_groups=mesh['video'=4,'tm'=16,'space'=4] {'space'}, use_global_device_ids=true, to_apply=%region_9.10 | all-reduce | flops 1536 | bytes 12288 | tf_op jit(solution)/shard_map/psum | solution.py:77
  316.9 15.6 %all-reduce.4.cloned.1.call-done = f32[1,512,128]{2,1,0:T(8,128)} async-done(((f32[1,512,128]{2,1,0:T(8,128)}), f32[1,512,128]{2,1,0:T(8,128)}) %all-reduce.4.cloned.1.call-update) | async-done | bytes 262160 | tf_op jit(solution)/shard_map/psum | solution.py:77
  333.7 4.7 collective-permute-start.1
  338.4 3.1 collective-permute-start
  342.2 1.2 collective-permute-done
  343.8 2.4 stack.26
  346.2 9.5 %all-to-all-start = ((f32[16,1,512,128]{3,2,1,0:T(8,128)}), f32[16,1,512,128]{3,2,1,0:T(8,128)}, u32[]{:S(2)}, u32[]{:S(2)}) async-start(f32[16,1,512,128]{3,2,1,0:T(8,128)} %stack.26), calls=%async_computation | async-start | bytes 8388608 | tf_op jit(solution)/shard_map/all_to_all | solution.py:103
  355.7 104.4 %all-gather = f32[16,1,128]{2,1,0:T(1,128)S(1)} all-gather(f32[1,1,128]{2,1,0:T(1,128)S(1)} %bitcast.74), channel_id=1, replica_groups=mesh['video'=4,'tm'=16,'space'=4] {'tm'}, dimensions={0}, use_global_device_ids=true | all-gather | bytes 8704 | tf_op jit(solution)/shard_map/all_gather | solution.py:101
  460.1 19.0 %while.14 = (s32[]{:T(128)}, f32[512,128]{1,0:T(8,128)S(1)}, s32[]{:T(128)}, f32[16,128]{1,0:T(8,128)S(1)}, f32[16,512,128]{2,1,0:T(8,128)}, /*index=5*/s32[]{:T(128)}, s32[]{:T(128)}) while((s32[]{:T(128)}, f32[512,128]{1,0:T(8,128)S(1)}, s32[]{:T(128)}, f32[16,128]{1,0:T(8,128)S(1)}, f32[16,512,128]{2,1,0:T(8,128)}, ...), condition=%wide.region_12.13_spmd.clone, body=%wide.region_11.12_spmd.clone.sunk | while | flops 262148 | bytes 788081 | solution.py:112
  461.3 1.1 fusion.57
  464.9 1.1 fusion.57
  468.5 1.1 fusion.57
  469.7 1.1 fusion.57
  472.0 1.1 fusion.57
  473.2 1.1 fusion.57
  476.8 1.1 fusion.57
  (57 shorter events, 15.6 us)
Async XLA Ops:
  6.5 1.6 copy-start
  6.5 326.1 %all-reduce.4.cloned.1.call-start = ((), (), s32[]{:S(2)}) async-start(), calls=%async_computation.1 | async-start | bytes 524288 | tf_op jit(solution)/shard_map/psum | solution.py:77
  301.2 8.1 %copy-start.1 = (f32[1,128]{1,0:T(1,128)S(1)}, f32[1,128]{1,0:T(1,128)}, u32[]{:S(2)}) copy-start(f32[1,128]{1,0:T(1,128)} %param.14) | copy-start | bytes 1540
  301.2 15.7 %copy-start.2 = (f32[3,128]{1,0:T(4,128)S(1)}, f32[3,128]{1,0:T(4,128)}, u32[]{:S(2)}) copy-start(f32[3,128]{1,0:T(4,128)} %param.15) | copy-start | bytes 4612
  301.2 42.3 %copy-start.4 = (bf16[128,128]{1,0:T(8,128)(2,1)S(1)}, bf16[128,128]{1,0:T(8,128)(2,1)}, u32[]{:S(2)}) copy-start(bf16[128,128]{1,0:T(8,128)(2,1)} %param.16) | copy-start | bytes 98308
  301.2 177.9 %copy-start.3 = (f32[2,128]{1,0:T(2,128)S(1)}, f32[2,128]{1,0:T(2,128)}, u32[]{:S(2)}) copy-start(f32[2,128]{1,0:T(2,128)} %param.17) | copy-start | bytes 3076
  333.7 8.5 %collective-permute-start.1 = (bf16[1,512,128]{2,1,0:T(8,128)(2,1)S(1)}, bf16[1,512,128]{2,1,0:T(8,128)(2,1)S(1)}, u32[]{:S(2)}, u32[]{:S(2)}) collective-permute-start(bf16[1,512,128]{2,1,0:T(8,128)(2,1)S(1)} %divide_convert_fusion), channel_id=1, source_target_pairs={{4,0},{8,4},{12,8},{16,12},{20,16},{24,20},{28,24},{32,28},{36,32}... | collective-permute-start | bytes 393224 | tf_op jit(solution)/shard_map/ppermute | solution.py:18
  338.4 5.0 %collective-permute-start = (bf16[1,512,128]{2,1,0:T(8,128)(2,1)S(1)}, bf16[1,512,128]{2,1,0:T(8,128)(2,1)S(1)}, u32[]{:S(2)}, u32[]{:S(2)}) collective-permute-start(bf16[1,512,128]{2,1,0:T(8,128)(2,1)S(1)} %divide_convert_fusion), channel_id=1, source_target_pairs={{0,4},{4,8},{8,12},{12,16},{16,20},{20,24},{24,28},{28,32},{32,36}... | collective-permute-start | bytes 393224 | tf_op jit(solution)/shard_map/ppermute | solution.py:16
  346.2 114.0 %all-to-all-start = ((f32[16,1,512,128]{3,2,1,0:T(8,128)}), f32[16,1,512,128]{3,2,1,0:T(8,128)}, u32[]{:S(2)}, u32[]{:S(2)}) async-start(f32[16,1,512,128]{3,2,1,0:T(8,128)} %stack.26), calls=%async_computation | async-start | bytes 8388608 | tf_op jit(solution)/shard_map/all_to_all | solution.py:103
Sparse Core Ops, SparseCore 0:
  285.6 46.9 all-reduce.3
